TPU v7x, 32 devices: a whole 2x2x4 slice. The times are simulated.
32 devices in a mesh: wide: 16 (over z, y, x), narrow: 2 (over core).
Axes of the slice: x: 2, y: 2, z: 4, core: 2. Of those that a mesh axis runs over, the one named last changes fastest.
Arguments:
- t_amps: bfloat16 [512, 32768], P('wide', 'narrow'), may hold values from -6 to 6
- v_blocks: bfloat16 [2, 16, 64, 128, 128], P('narrow', 'wide'), may hold values from -0.25 to 0.25
- block_pos: int32 [2, 16, 64], P('narrow', 'wide'), may hold values from 0 to 2047, as said below
- block_count: int32 [2, 16], P('narrow', 'wide'), may hold values from 24 to 64, as said below
Outputs:
- ladder: float32 [512, 32768], P('narrow', 'wide')
Inputs may be any that keep to these rules, and one draw needn't show every extreme that they name: `block_pos`: within one tile the places of all 64 slots are distinct, and they lie in at most 64 distinct block rows. `block_count`: some tile holds exactly 64 stored blocks; loads are skewed, most tiles holding far fewer.
All inputs are finite; a program needn't handle non-finite values.
Results may differ from a plain program's by a relative error of at most 0.0003.
Values may be sent and summed in bfloat16 or wider, within the bound.
A program may use at most 320 MiB of HBM per device.

v0:
```python
import jax
import jax.numpy as jnp
from jax import lax
from jax.sharding import PartitionSpec as P

W = 32768


def shards(t_amps, v_blocks, block_pos, block_count):
    stored = v_blocks[0, 0]
    places = block_pos[0, 0]
    slot_count = block_count[0, 0]
    block_size = stored.shape[1]
    slot_total = stored.shape[0]
    row_blocks = t_amps.shape[1] // block_size
    col_blocks = W // (lax.axis_size("wide") * block_size)
    live_mask = (jnp.arange(slot_total, dtype=jnp.int32) < slot_count).astype(jnp.bfloat16)
    masked = stored * live_mask[:, None, None]
    row_of = places // col_blocks
    col_of = places % col_blocks

    def build_product(panel_blocks, slot_rows):
        dense_places = slot_rows * col_blocks + col_of
        dense_tile = jnp.zeros((panel_blocks * col_blocks, block_size, block_size), jnp.bfloat16)
        dense_tile = dense_tile.at[dense_places].add(masked)
        dense_tile = dense_tile.reshape(panel_blocks, col_blocks, block_size, block_size)
        dense_tile = jnp.transpose(dense_tile, (0, 2, 1, 3)).reshape(
            panel_blocks * block_size, col_blocks * block_size
        )

        def product(t_rows):
            return jnp.dot(t_rows, dense_tile, preferred_element_type=jnp.float32)

        return product

    product = build_product(row_blocks, row_of)
    gathered = lax.all_gather(t_amps, "wide", axis=0, tiled=True)
    partial_sum = product(gathered)
    return lax.psum_scatter(partial_sum, "narrow", scatter_dimension=0, tiled=True)


def solution(mesh):
    in_specs = (
        P("wide", "narrow"),
        P("narrow", "wide", None, None, None),
        P("narrow", "wide", None),
        P("narrow", "wide"),
    )
    out_specs = P("narrow", "wide")
    return jax.shard_map(shards, mesh=mesh, in_specs=in_specs, out_specs=out_specs, check_vma=False)
```

profile of v0, /device:TPU:1, one launch (start us, length us, event | category | flops | bytes accessed | tf_op | source)
XLA Modules:
  0.0 281.0 jit_solution(2076956381307750412)
XLA Ops:
  6.5 0.0 all-gather.2.cloned.1.call-start
  6.5 0.7 all-gather.2.cloned.1.call-update
  7.3 0.0 reduce-scatter.2.cloned.1.call-start
  8.0 0.7 fusion.7
  8.6 1.8 bitcast_multiply_fusion
  10.4 22.0 %broadcast_in_dim.2 = bf16[2048,128,128]{2,1,0:T(8,128)(2,1)} broadcast(bf16[]{:T(256)} %constant.26.clone.1), dimensions={} | broadcast | bytes 67108864 | tf_op jit(solution)/shard_map/broadcast_in_dim | solution.py:24
  32.5 12.4 %scatter_fusion = bf16[2048,128,128]{2,1,0:T(8,128)(2,1)} fusion(bf16[2048,128,128]{2,1,0:T(8,128)(2,1)} %broadcast_in_dim.2, s32[64]{0:T(128)S(1)} %fusion.7, bf16[64,128,128]{2,1,0:T(8,128)(2,1)S(1)} %bitcast_multiply_fusion), kind=kCustom, calls=%fused_computation | custom fusion | flops 1048576 | bytes 6291712 | tf_op jit(solution)/shard_map/scatter-add | solution.py:25
  44.9 57.7 %copy.7 = bf16[128,128,16,128]{3,2,1,0:T(8,128)(2,1)} copy(bf16[128,128,16,128]{3,1,2,0:T(8,128)(2,1)} %bitcast.5) | data formatting | bytes 134217728 | tf_op jit(solution)/shard_map/transpose | solution.py:27
  102.6 99.9 %all-gather.2.cloned.1.call-done = bf16[512,16384]{1,0:T(8,128)(2,1)} async-done(((bf16[32,16384]{1,0:T(8,128)(2,1)}), bf16[512,16384]{1,0:T(8,128)(2,1)}) %all-gather.2.cloned.1.call-update) | async-done | bytes 16777232 | tf_op jit(solution)/shard_map/all_gather | solution.py:37
  202.5 57.3 %fusion.3 = f32[512,2048]{0,1:T(8,128)} fusion(bf16[512,16384]{1,0:T(8,128)(2,1)} %all-gather.2.cloned.1.call-done, bf16[2048,8,16,128]{3,2,1,0:T(8,128)(2,1)} %bitcast.9), kind=kOutput, calls=%fused_computation.4 | convolution fusion | flops 34359738368 | bytes 88080384 | tf_op jit(solution)/shard_map/dot_general | solution.py:32
  259.8 0.0 reduce-scatter.2.cloned.1.call-update
  259.8 11.4 %reduce-scatter.2.cloned.1.call-done = f32[256,2048]{0,1:T(8,128)} async-done(((f32[512,2048]{0,1:T(8,128)}), f32[256,2048]{0,1:T(8,128)}) %reduce-scatter.2.cloned.1.call-update) | async-done | bytes 2097168 | tf_op jit(solution)/shard_map/reduce_scatter | solution.py:39
  271.3 2.9 %copy.8 = f32[256,2048]{1,0:T(8,128)} copy(f32[256,2048]{0,1:T(8,128)} %reduce-scatter.2.cloned.1.call-done) | data formatting | bytes 4194304 | tf_op jit(solution)/shard_map/reduce_scatter | solution.py:39
  (1 shorter events, 0.0 us)
Async XLA Ops:
  6.5 195.9 %all-gather.2.cloned.1.call-start = ((), (), s32[]{:S(2)}) async-start(), calls=%async_computation.1 | async-start | bytes 17825792 | tf_op jit(solution)/shard_map/all_gather | solution.py:37
  7.3 264.0 %reduce-scatter.2.cloned.1.call-start = ((), (), s32[]{:S(2)}) async-start(), calls=%async_computation.2 | async-start | bytes 6291456 | tf_op jit(solution)/shard_map/reduce_scatter | solution.py:39
Sparse Core Ops, SparseCore 0:
  10.1 192.3 all-gather.1
  259.9 11.2 reduce-scatter.1
where the time goes:
time: 282 us; the launch traced here: 281 us
  waiting for transfers between devices  112 us (40%)
  local copies, waits for them, and re-layouts  82.6 us (29%)
  matrix products  57.3 us (20%)
  other arithmetic  14.9 us (5%)
  between operations  14.1 us (5%)
    all_gather x1, waiting for transfers between devices, shards(): gathered = lax.all_gather(t_amps, 'wide', axis=0, tiled=True)  99.9 us
    transpose x1, local copies, waits for them, and re-layouts, build_product(): jnp.transpose(dense_tile, (0, 2, 1, 3))  57.7 us
    dot_general x1, matrix products, product(): return jnp.dot(t_rows, dense_tile, preferred_element_type=jnp.float32)  57.3 us
    broadcast_in_dim x1, local copies, waits for them, and re-layouts, build_product(): jnp.zeros((panel_blocks * col_blocks, block_size, block_size), jnp.bfloat16)  22 us
    scatter-add x1, other arithmetic, build_product(): dense_tile = dense_tile.at[dense_places].add(masked)  12.4 us
    reduce_scatter x1, waiting for transfers between devices, shards(): lax.psum_scatter(partial_sum, 'narrow', scatter_dimension=0, tiled=True)  11.4 us
  transfers between devices with their start and end apart: 2, of which 2 were waited for; matrix products, arithmetic and copies ran while one was open for 34% of the time, Pallas kernels for 0%

commit v1 on v0

v1 whole, which is shorter than its diff:
```python
import functools

import jax
import jax.numpy as jnp
from jax import lax
from jax.experimental import pallas as pl
from jax.experimental.pallas import tpu as pltpu
from jax.sharding import PartitionSpec as P

MESH = pl.DeviceIdType.MESH


def dense_shards(width, t_amps, v_blocks, block_pos, block_count):
    stored = v_blocks[0, 0]
    places = block_pos[0, 0]
    slot_count = block_count[0, 0]
    block_size = stored.shape[1]
    slot_total = stored.shape[0]
    row_blocks = t_amps.shape[1] // block_size
    col_blocks = width // (lax.axis_size("wide") * block_size)
    live_mask = (jnp.arange(slot_total, dtype=jnp.int32) < slot_count).astype(jnp.bfloat16)
    masked = stored * live_mask[:, None, None]
    dense_tile = jnp.zeros((row_blocks * col_blocks, block_size, block_size), jnp.bfloat16)
    dense_tile = dense_tile.at[places].add(masked)
    dense_tile = dense_tile.reshape(row_blocks, col_blocks, block_size, block_size)
    dense_tile = jnp.transpose(dense_tile, (0, 2, 1, 3)).reshape(row_blocks * block_size, col_blocks * block_size)
    gathered = lax.all_gather(t_amps, "wide", axis=0, tiled=True)
    partial_sum = jnp.dot(gathered, dense_tile, preferred_element_type=jnp.float32)
    return lax.psum_scatter(partial_sum, "narrow", scatter_dimension=0, tiled=True)


def ladder_kernel(depth, t, v_tile, meta_v, out, *scratch):
    bufs = scratch[: 2 * depth - 1]
    (v_own, v_other, meta_in, meta, meta_other, runs, part, core_in, y_out, local_sem, az_send, az_recv, bz_send, bz_recv,
     ax_send, ax_recv, one_send, one_recv, core_send, core_recv, y_send, y_recv) = scratch[2 * depth - 1:]
    wide, core = lax.axis_index("wide"), lax.axis_index("narrow")
    z, y, x = wide // 4, (wide // 2) % 2, wide % 2
    up, down = (wide + 4, core), (wide - 4, core)
    across = (wide + 1 - 2 * x, core)
    beside = (wide + 2 - 4 * y, core)
    twin = (wide, 1 - core)
    half = depth // 2
    row_blocks, rows, unused = t.shape
    v = v_tile.at[0, 0]
    slots, size = v.shape[0], v.shape[1]
    col_blocks = out.shape[-1] // size
    second = row_blocks * 5 // 32
    first = row_blocks - second
    first_cols, second_cols = pl.ds(0, first), pl.ds(first, second)
    has_up, has_down = z < depth - 1, z > 0

    def copy(src, dst, send, recv, device):
        return pltpu.make_async_remote_copy(
            src_ref=src, dst_ref=dst, send_sem=send, recv_sem=recv, device_id=device, device_id_type=MESH
        )

    def place(b):
        if b == 0:
            return z, None
        if b < depth:
            return z - b, z >= b
        return z + (b - depth + 1), z + (b - depth + 1) < depth

    def guarded(cond, fn):
        if cond is None:
            fn()
        else:
            pl.when(cond)(fn)

    def both(a, b):
        return b if a is None else a if b is None else jnp.logical_and(a, b)

    def from_own(cols):
        return t.at[cols]

    def hops(b):
        moves = []
        if b < depth - 1:
            moves.append((b + 1, up, has_up, b))
        if b == 0 or depth <= b < 2 * depth - 2:
            landing = depth if b == 0 else b + 1
            moves.append((landing, down, has_down, depth - 1 + (landing - depth)))
        return moves

    def az(b, move):
        landing, device, unused, sem = move
        src = from_own(first_cols) if b == 0 else bufs[b].at[x, first_cols]
        return copy(src, bufs[landing].at[x, first_cols], az_send.at[sem], az_recv.at[landing], device)

    def bz(b, move):
        landing, device, unused, sem = move
        return copy(bufs[b].at[:, second_cols], bufs[landing].at[:, second_cols], bz_send.at[sem], bz_recv.at[landing], device)

    def ax(b):
        src = from_own(first_cols) if b == 0 else bufs[b].at[x, first_cols]
        return copy(src, bufs[b].at[x, first_cols], ax_send.at[b], ax_recv.at[b], across)

    def az_wait(b):
        dst = bufs[b].at[x, first_cols]
        copy(dst, dst, az_send.at[0], az_recv.at[b], up).wait_recv()

    def bz_wait(b):
        dst = bufs[b].at[:, second_cols]
        copy(dst, dst, bz_send.at[0], bz_recv.at[b], up).wait_recv()

    def ax_wait(b):
        dst = bufs[b].at[1 - x, first_cols]
        copy(dst, dst, ax_send.at[b], ax_recv.at[b], across).wait_recv()

    barrier = pltpu.get_barrier_semaphore()
    for device in (across, beside, twin):
        pl.semaphore_signal(barrier, inc=1, device_id=device, device_id_type=MESH)
    pl.when(has_up)(lambda: pl.semaphore_signal(barrier, inc=1, device_id=up, device_id_type=MESH))
    pl.when(has_down)(lambda: pl.semaphore_signal(barrier, inc=1, device_id=down, device_id_type=MESH))
    pl.semaphore_wait(barrier, 3 + has_up.astype(jnp.int32) + has_down.astype(jnp.int32))

    bx = copy(from_own(second_cols), bufs[0].at[x, second_cols], one_send.at[0], one_recv.at[0], across)
    vy = copy(v, v_other, one_send.at[1], one_recv.at[1], beside)
    my = copy(meta_v, meta_in, one_send.at[2], one_recv.at[2], beside)
    bx.start()
    for move in hops(0):
        guarded(move[2], lambda move=move: az(0, move).start())
    ax(0).start()
    my.start()
    vy.start()
    own_t = pltpu.make_async_copy(t, bufs[0].at[x], local_sem.at[0])
    own_v = pltpu.make_async_copy(v, v_own, local_sem.at[1])
    own_t.start()
    own_v.start()
    own_m = pltpu.make_async_copy(meta_v, meta, local_sem.at[3])
    own_m.start()
    own_m.wait()
    own_t.wait()
    bx.wait_recv()
    for move in hops(0):
        guarded(move[2], lambda move=move: bz(0, move).start())

    def forward(b):
        def run():
            az_wait(b)
            for move in hops(b):
                guarded(move[2], lambda move=move: az(b, move).start())
            ax(b).start()
            bz_wait(b)
            for move in hops(b):
                guarded(move[2], lambda move=move: bz(b, move).start())

        guarded(place(b)[1], run)

    def products(b, strip, stored, info):
        zp = place(b)[0]

        def slot(s, carry):
            at_row = info[1, s]
            left = jnp.concatenate([bufs[b][0, at_row], bufs[b][1, at_row]], axis=0)
            new = jnp.dot(left, stored[info[0, s]], preferred_element_type=jnp.float32)
            runs[s + 1] = new + runs[s] * info[2, s].astype(jnp.float32)
            return carry

        runs[0] = jnp.zeros((2 * rows, size), jnp.float32)
        lax.fori_loop(0, slots, slot, 0, unroll=8)
        for c in range(col_blocks):
            value = runs[info[3, c] + 1] * info[4, c].astype(jnp.float32)
            part[zp, strip, :, c * size:(c + 1) * size] = value

    def core_copy(b, strip):
        zp = place(b)[0]
        return copy(part.at[zp, strip], core_in.at[zp % half, strip], core_send.at[b, strip], core_recv.at[b, strip], twin)

    def out_rows(b):
        return pl.ds(pl.multiple_of((place(b)[0] % half * 2 + y) * 2 * rows, 2 * rows), 2 * rows)

    def y_copy(b):
        return copy(y_out.at[place(b)[0] % half], out.at[out_rows(b), :], y_send.at[b], y_recv.at[b], beside)

    def mine(b):
        return place(b)[0] // half == core

    def compute(b):
        def run():
            ax_wait(b)
            for strip, stored, info in ((0, v_other, meta_other), (1, v_own, meta)):
                products(b, strip, stored, info)
                pl.when(jnp.logical_not(mine(b)))(lambda strip=strip: core_copy(b, strip).start())

        guarded(place(b)[1], run)

    def finish(b):
        def run():
            zp = place(b)[0]
            slot = zp % half
            core_copy(b, 0).wait_recv()
            y_out[slot] = part[zp, 0] + core_in[slot, 0]
            y_copy(b).start()
            core_copy(b, 1).wait_recv()
            out[out_rows(b), :] = part[zp, 1] + core_in[slot, 1]

        guarded(both(place(b)[1], mine(b)), run)

    def at(k):
        return [0] if k == 0 else [k, depth - 1 + k]

    ready = done = 0
    for k in range(1, depth):
        for b in at(k):
            forward(b)
        if k == min(2, depth - 1):
            own_v.wait()
            my.wait_recv()
            into = pltpu.make_async_copy(meta_in, meta_other, local_sem.at[2])
            into.start()
            into.wait()
            vy.wait_recv()
        if k >= 2:
            while ready < (depth - 1 if k == depth - 1 else k - 1):
                for b in at(ready):
                    compute(b)
                ready += 1
                if ready - 2 >= done:
                    for b in at(done):
                        finish(b)
                    done += 1
    while ready < depth:
        for b in at(ready):
            compute(b)
        ready += 1
    while done < depth:
        for b in at(done):
            finish(b)
        done += 1

    bx.wait_send()
    vy.wait_send()
    my.wait_send()
    for b in range(2 * depth - 1):
        valid = place(b)[1]
        for move in hops(b):
            guarded(both(valid, move[2]), lambda b=b, move=move: (az(b, move).wait_send(), bz(b, move).wait_send(), None)[-1])
        guarded(valid, lambda b=b: ax(b).wait_send())
        other = jnp.logical_not(mine(b))
        guarded(both(valid, other), lambda b=b: (core_copy(b, 0).wait_send(), core_copy(b, 1).wait_send(), None)[-1])
        guarded(both(valid, mine(b)), lambda b=b: y_copy(b).wait())


def slot_table(places, count, col_blocks):
    total = places.shape[0]
    ids = jnp.arange(total, dtype=jnp.int32)
    cols = jnp.where(ids < count, places % col_blocks, col_blocks)
    key = cols * total + ids
    rank = jnp.sum((key[None, :] < key[:, None]).astype(jnp.int32), axis=1)
    hit = (rank[:, None] == ids[None, :]).astype(jnp.int32)
    order = jnp.sum(hit * ids[:, None], axis=0)
    row = jnp.sum(hit * (places // col_blocks)[:, None], axis=0)
    col = jnp.sum(hit * cols[:, None], axis=0)
    before = jnp.sum((rank[:, None] + 1 == ids[None, :]).astype(jnp.int32) * (cols + 1)[:, None], axis=0) - 1
    same = (col == before).astype(jnp.int32)
    each = jnp.arange(col_blocks, dtype=jnp.int32)
    last = jnp.sum((cols[None, :] <= each[:, None]).astype(jnp.int32), axis=1) - 1
    some = jnp.sum((cols[None, :] == each[:, None]).astype(jnp.int32), axis=1)
    lanes = -(-max(total, col_blocks) // 128) * 128

    def wide(a):
        return jnp.pad(a, (0, lanes - a.shape[0]))

    zero = jnp.zeros((lanes,), jnp.int32)
    return jnp.stack([wide(order), wide(row), wide(same), wide(jnp.maximum(last, 0)), wide(jnp.minimum(some, 1)), zero, zero, zero])


def ring_shards(width, wide_size, t_amps, v_blocks, block_pos, block_count):
    rows, columns = t_amps.shape
    slots, size = v_blocks.shape[2], v_blocks.shape[3]
    depth = wide_size // 4
    half, buffers = depth // 2, 2 * depth - 1
    strip = width // wide_size
    meta = slot_table(block_pos[0, 0], block_count[0, 0], strip // size)
    by_block = jnp.transpose(t_amps.reshape(rows, columns // size, size), (1, 0, 2))
    bf16, f32, i32 = jnp.bfloat16, jnp.float32, jnp.int32
    dma = pltpu.SemaphoreType.DMA
    out = pl.pallas_call(
        functools.partial(ladder_kernel, depth),
        out_shape=jax.ShapeDtypeStruct((half * 4 * rows, strip), f32),
        in_specs=[
            pl.BlockSpec(memory_space=pl.ANY),
            pl.BlockSpec(memory_space=pl.ANY),
            pl.BlockSpec(memory_space=pltpu.VMEM),
        ],
        out_specs=pl.BlockSpec(memory_space=pltpu.VMEM),
        scratch_shapes=[pltpu.VMEM((2, columns // size, rows, size), bf16)] * buffers + [
            pltpu.VMEM((slots, size, size), bf16),
            pltpu.VMEM((slots, size, size), bf16),
            pltpu.VMEM(meta.shape, i32),
            pltpu.SMEM(meta.shape, i32),
            pltpu.SMEM(meta.shape, i32),
            pltpu.VMEM((slots + 1, 2 * rows, size), f32),
            pltpu.VMEM((depth, 2, 2 * rows, strip), f32),
            pltpu.VMEM((half, 2, 2 * rows, strip), f32),
            pltpu.VMEM((half, 2 * rows, strip), f32),
            dma((4,)),
            dma((2 * depth,)), dma((buffers,)),
            dma((2 * depth,)), dma((buffers,)),
            dma((buffers,)), dma((buffers,)),
            dma((3,)), dma((3,)),
            dma((buffers, 2)), dma((buffers, 2)),
            dma((buffers,)), dma((buffers,)),
        ],
        compiler_params=pltpu.CompilerParams(
            collective_id=0, has_side_effects=True, vmem_limit_bytes=56 * 1024 * 1024
        ),
    )(by_block, v_blocks, meta)
    return out


def solution(mesh):
    in_specs = (
        P("wide", "narrow"),
        P("narrow", "wide", None, None, None),
        P("narrow", "wide", None),
        P("narrow", "wide"),
    )
    out_specs = P("narrow", "wide")
    wide_size, narrow_size = mesh.shape["wide"], mesh.shape["narrow"]

    def program(t_amps, v_blocks, block_pos, block_count):
        width = t_amps.shape[1]
        if narrow_size == 2 and wide_size % 8 == 0:
            body = functools.partial(ring_shards, width, wide_size)
        else:
            body = functools.partial(dense_shards, width)
        run = jax.shard_map(body, mesh=mesh, in_specs=in_specs, out_specs=out_specs, check_vma=False)
        return run(t_amps, v_blocks, block_pos, block_count)

    return program
```

time: 282 us -> 122 us (0.43)
  Pallas kernels: 0 us -> 115 us
  waiting for transfers between devices: 112 us -> 0 us
  local copies, waits for them, and re-layouts: 82.6 us -> 4.93 us
  matrix products: 57.3 us -> 0 us
  other arithmetic: 14.9 us -> 1.12 us
  between operations: 14.1 us -> 0.82 us
    pallas_call x0 -> x1, Pallas kernels: none -> 115 us  [ring_shards(): pl.pallas_call(functools.partial(ladder_kernel, depth), out_shape=jax.Sha...]
    all_gather x1 -> x0, waiting for transfers between devices: 99.9 us -> none  [shards(): gathered = lax.all_gather(t_amps, 'wide', axis=0, tiled=True)]
    dot_general x1 -> x0, matrix products: 57.3 us -> none  [product(): return jnp.dot(t_rows, dense_tile, preferred_element_type=jnp.float32)]
    transpose x1, local copies, waits for them, and re-layouts: 57.7 us -> 1.15 us  [ring_shards(): jnp.transpose(t_amps.reshape(rows, columns // size, size), (1, 0, 2))]
    broadcast_in_dim x1 -> x0, local copies, waits for them, and re-layouts: 22 us -> none  [build_product(): jnp.zeros((panel_blocks * col_blocks, block_size, block_size), jnp.bfloat16)]
    scatter-add x1 -> x0, other arithmetic: 12.4 us -> none  [build_product(): dense_tile = dense_tile.at[dense_places].add(masked)]
    reduce_scatter x1 -> x0, waiting for transfers between devices: 11.4 us -> none  [shards(): lax.psum_scatter(partial_sum, 'narrow', scatter_dimension=0, tiled=True)]
    unnamed x0 -> x3, local copies, waits for them, and re-layouts: none -> 3.14 us
  transfers between devices with their start and end apart: 2 -> 0, of which waited for: 2 -> 0; matrix products, arithmetic and copies ran while one was open for 34% -> 0% of each run, Pallas kernels for 0% -> 0%
where the time goes in v1:
time: 122 us
  Pallas kernels  115 us (94%)
  local copies, waits for them, and re-layouts  4.93 us (4%)
    pallas_call x1, Pallas kernels, ring_shards(): pl.pallas_call(functools.partial(ladder_kernel, depth), out_shape=jax.Sha...  115 us
    unnamed x3, local copies, waits for them, and re-layouts  3.14 us

profile of v1, /device:TPU:1, one launch (start us, length us, event | category | flops | bytes accessed | tf_op | source)
XLA Modules:
  0.0 121.5 jit_solution(16098606752883279913)
XLA Ops:
  0.0 0.0 copy-start
  0.7 0.7 broadcast_add_fusion
  1.4 0.2 convert_reduce_fusion
  1.6 0.1 select_reduce_fusion.1
  1.8 0.1 convert_reduce_fusion.1
  2.0 0.6 stack.31.meta_v
  2.6 0.0 copy-done
  2.6 1.1 bitcast_bitcast_fusion.t
  3.7 114.7 %shard_map.46 = f32[256,2048]{1,0:T(8,128)} custom-call(bf16[128,32,128]{2,1,0:T(8,128)(2,1)} %bitcast_bitcast_fusion.t, bf16[1,1,64,128,128]{4,3,2,1,0:T(8,128)(2,1)} %v_tile.1, s32[8,128]{1,0:T(8,128)} %stack.31.meta_v), custom_call_target="tpu_custom_call" | custom-call | tf_op jit(solution)/shard_map/pallas_call | solution.py:279
  118.4 3.1 %copy.11 = f32[256,2048]{1,0:T(8,128)} copy(f32[256,2048]{1,0:T(8,128)} %shard_map.46) | data formatting | bytes 4194304
  (11 shorter events, 0.1 us)
Async XLA Ops:
  0.0 2.6 %copy-start = (bf16[32,16384]{1,0:T(8,128)(2,1)S(1)}, bf16[32,16384]{1,0:T(8,128)(2,1)}, u32[]{:S(2)}) copy-start(bf16[32,16384]{1,0:T(8,128)(2,1)} %param.4) | copy-start | bytes 3145732

commit v2 on v1

--- a/solution.py
+++ b/solution.py
@@ -8,6 +8,7 @@
 from jax.sharding import PartitionSpec as P
 
 MESH = pl.DeviceIdType.MESH
+PIECES = 2
 
 
 def dense_shards(width, t_amps, v_blocks, block_pos, block_count):
@@ -46,7 +47,9 @@
     col_blocks = out.shape[-1] // size
     second = row_blocks * 5 // 32
     first = row_blocks - second
-    first_cols, second_cols = pl.ds(0, first), pl.ds(first, second)
+    cuts = [first * q // PIECES for q in range(PIECES + 1)]
+    pieces = [pl.ds(cuts[q], cuts[q + 1] - cuts[q]) for q in range(PIECES)]
+    second_cols = pl.ds(first, second)
     has_up, has_down = z < depth - 1, z > 0
 
     def copy(src, dst, send, recv, device):
@@ -82,30 +85,31 @@
             moves.append((landing, down, has_down, depth - 1 + (landing - depth)))
         return moves
 
-    def az(b, move):
+    def az(b, move, q):
         landing, device, unused, sem = move
-        src = from_own(first_cols) if b == 0 else bufs[b].at[x, first_cols]
-        return copy(src, bufs[landing].at[x, first_cols], az_send.at[sem], az_recv.at[landing], device)
+        src = from_own(pieces[q]) if b == 0 else bufs[b].at[x, pieces[q]]
+        return copy(src, bufs[landing].at[x, pieces[q]], az_send.at[sem, q], az_recv.at[landing, q], device)
 
     def bz(b, move):
         landing, device, unused, sem = move
         return copy(bufs[b].at[:, second_cols], bufs[landing].at[:, second_cols], bz_send.at[sem], bz_recv.at[landing], device)
 
-    def ax(b):
-        src = from_own(first_cols) if b == 0 else bufs[b].at[x, first_cols]
-        return copy(src, bufs[b].at[x, first_cols], ax_send.at[b], ax_recv.at[b], across)
-
-    def az_wait(b):
-        dst = bufs[b].at[x, first_cols]
-        copy(dst, dst, az_send.at[0], az_recv.at[b], up).wait_recv()
+    def ax(b, q):
+        src = from_own(pieces[q]) if b == 0 else bufs[b].at[x, pieces[q]]
+        return copy(src, bufs[b].at[x, pieces[q]], ax_send.at[b, q], ax_recv.at[b, q], across)
+
+    def az_wait(b, q):
+        dst = bufs[b].at[x, pieces[q]]
+        copy(dst, dst, az_send.at[0, q], az_recv.at[b, q], up).wait_recv()
 
     def bz_wait(b):
         dst = bufs[b].at[:, second_cols]
         copy(dst, dst, bz_send.at[0], bz_recv.at[b], up).wait_recv()
 
     def ax_wait(b):
-        dst = bufs[b].at[1 - x, first_cols]
-        copy(dst, dst, ax_send.at[b], ax_recv.at[b], across).wait_recv()
+        for q in range(PIECES):
+            dst = bufs[b].at[1 - x, pieces[q]]
+            copy(dst, dst, ax_send.at[b, q], ax_recv.at[b, q], across).wait_recv()
 
     barrier = pltpu.get_barrier_semaphore()
     for device in (across, beside, twin):
@@ -118,9 +122,10 @@
     vy = copy(v, v_other, one_send.at[1], one_recv.at[1], beside)
     my = copy(meta_v, meta_in, one_send.at[2], one_recv.at[2], beside)
     bx.start()
-    for move in hops(0):
-        guarded(move[2], lambda move=move: az(0, move).start())
-    ax(0).start()
+    for q in range(PIECES):
+        for move in hops(0):
+            guarded(move[2], lambda move=move, q=q: az(0, move, q).start())
+        ax(0, q).start()
     my.start()
     vy.start()
     own_t = pltpu.make_async_copy(t, bufs[0].at[x], local_sem.at[0])
@@ -132,15 +137,22 @@
     own_m.wait()
     own_t.wait()
     bx.wait_recv()
-    for move in hops(0):
-        guarded(move[2], lambda move=move: bz(0, move).start())
-
-    def forward(b):
+
+    def second_own(k):
+        for move, turn in zip(hops(0), (z, depth - 1 - z)):
+            guarded(both(move[2], turn == k), lambda move=move: bz(0, move).start())
+
+    def forward(b, q):
         def run():
-            az_wait(b)
+            az_wait(b, q)
             for move in hops(b):
-                guarded(move[2], lambda move=move: az(b, move).start())
-            ax(b).start()
+                guarded(move[2], lambda move=move: az(b, move, q).start())
+            ax(b, q).start()
+
+        guarded(place(b)[1], run)
+
+    def forward_second(b):
+        def run():
             bz_wait(b)
             for move in hops(b):
                 guarded(move[2], lambda move=move: bz(b, move).start())
@@ -200,34 +212,28 @@
     def at(k):
         return [0] if k == 0 else [k, depth - 1 + k]
 
-    ready = done = 0
+    second_own(0)
+    for k in range(1, depth):
+        for q in range(PIECES):
+            for b in at(k):
+                forward(b, q)
+        second_own(k)
+    own_v.wait()
+    my.wait_recv()
+    into = pltpu.make_async_copy(meta_in, meta_other, local_sem.at[2])
+    into.start()
+    into.wait()
+    vy.wait_recv()
+    compute(0)
     for k in range(1, depth):
         for b in at(k):
-            forward(b)
-        if k == min(2, depth - 1):
-            own_v.wait()
-            my.wait_recv()
-            into = pltpu.make_async_copy(meta_in, meta_other, local_sem.at[2])
-            into.start()
-            into.wait()
-            vy.wait_recv()
-        if k >= 2:
-            while ready < (depth - 1 if k == depth - 1 else k - 1):
-                for b in at(ready):
-                    compute(b)
-                ready += 1
-                if ready - 2 >= done:
-                    for b in at(done):
-                        finish(b)
-                    done += 1
-    while ready < depth:
-        for b in at(ready):
+            forward_second(b)
+        for b in at(k - 1):
+            finish(b)
+        for b in at(k):
             compute(b)
-        ready += 1
-    while done < depth:
-        for b in at(done):
-            finish(b)
-        done += 1
+    for b in at(depth - 1):
+        finish(b)
 
     bx.wait_send()
     vy.wait_send()
@@ -235,8 +241,8 @@
     for b in range(2 * depth - 1):
         valid = place(b)[1]
         for move in hops(b):
-            guarded(both(valid, move[2]), lambda b=b, move=move: (az(b, move).wait_send(), bz(b, move).wait_send(), None)[-1])
-        guarded(valid, lambda b=b: ax(b).wait_send())
+            guarded(both(valid, move[2]), lambda b=b, move=move: [az(b, move, q).wait_send() for q in range(PIECES)] and bz(b, move).wait_send())
+        guarded(valid, lambda b=b: [ax(b, q).wait_send() for q in range(PIECES)] and None)
         other = jnp.logical_not(mine(b))
         guarded(both(valid, other), lambda b=b: (core_copy(b, 0).wait_send(), core_copy(b, 1).wait_send(), None)[-1])
         guarded(both(valid, mine(b)), lambda b=b: y_copy(b).wait())
@@ -296,9 +302,9 @@
             pltpu.VMEM((half, 2, 2 * rows, strip), f32),
             pltpu.VMEM((half, 2 * rows, strip), f32),
             dma((4,)),
+            dma((2 * depth, PIECES)), dma((buffers, PIECES)),
             dma((2 * depth,)), dma((buffers,)),
-            dma((2 * depth,)), dma((buffers,)),
-            dma((buffers,)), dma((buffers,)),
+            dma((buffers, PIECES)), dma((buffers, PIECES)),
             dma((3,)), dma((3,)),
             dma((buffers, 2)), dma((buffers, 2)),
             dma((buffers,)), dma((buffers,)),

time: 122 us -> 107 us (0.88)
  Pallas kernels: 115 us -> 99.8 us
    pallas_call x1, Pallas kernels: 115 us -> 99.8 us  [ring_shards(): pl.pallas_call(functools.partial(ladder_kernel, depth), out_shape=jax.Sha...]
where the time goes in v2:
time: 107 us
  Pallas kernels  99.8 us (93%)
  local copies, waits for them, and re-layouts  4.93 us (5%)
  other arithmetic  1.12 us (1%)
    pallas_call x1, Pallas kernels, ring_shards(): pl.pallas_call(functools.partial(ladder_kernel, depth), out_shape=jax.Sha...  99.8 us
    unnamed x3, local copies, waits for them, and re-layouts  3.14 us

profile of v2, /device:TPU:1, one launch (start us, length us, event | category | flops | bytes accessed | tf_op | source)
XLA Modules:
  0.0 106.6 jit_solution(10285605888376557840)
XLA Ops:
  0.0 0.0 copy-start
  0.7 0.7 broadcast_add_fusion
  1.4 0.2 convert_reduce_fusion
  1.6 0.1 select_reduce_fusion.1
  1.8 0.1 convert_reduce_fusion.1
  2.0 0.6 stack.31.meta_v
  2.6 0.0 copy-done
  2.6 1.1 %bitcast_bitcast_fusion.t = bf16[128,32,128]{2,1,0:T(8,128)(2,1)} fusion(bf16[32,16384]{1,0:T(8,128)(2,1)S(1)} %copy-done), kind=kLoop, calls=%fused_computation | loop fusion | bytes 2097152 | tf_op jit(solution)/shard_map/transpose | solution.py:282
  3.7 99.8 %shard_map.46 = f32[256,2048]{1,0:T(8,128)} custom-call(bf16[128,32,128]{2,1,0:T(8,128)(2,1)} %bitcast_bitcast_fusion.t, bf16[1,1,64,128,128]{4,3,2,1,0:T(8,128)(2,1)} %v_tile.1, s32[8,128]{1,0:T(8,128)} %stack.31.meta_v), custom_call_target="tpu_custom_call" | custom-call | tf_op jit(solution)/shard_map/pallas_call | solution.py:285
  103.5 3.1 %copy.11 = f32[256,2048]{1,0:T(8,128)} copy(f32[256,2048]{1,0:T(8,128)} %shard_map.46) | data formatting | bytes 4194304
  (11 shorter events, 0.1 us)
Async XLA Ops:
  0.0 2.6 %copy-start = (bf16[32,16384]{1,0:T(8,128)(2,1)S(1)}, bf16[32,16384]{1,0:T(8,128)(2,1)}, u32[]{:S(2)}) copy-start(bf16[32,16384]{1,0:T(8,128)(2,1)} %param.4) | copy-start | bytes 3145732

commit v3 on v2

v3 whole, which is shorter than its diff:
```python
import functools

import jax
import jax.numpy as jnp
from jax import lax
from jax.experimental import pallas as pl
from jax.experimental.pallas import tpu as pltpu
from jax.sharding import PartitionSpec as P

MESH = pl.DeviceIdType.MESH
PIECES = 2


def dense_shards(width, t_amps, v_blocks, block_pos, block_count):
    stored = v_blocks[0, 0]
    places = block_pos[0, 0]
    slot_count = block_count[0, 0]
    block_size = stored.shape[1]
    slot_total = stored.shape[0]
    row_blocks = t_amps.shape[1] // block_size
    col_blocks = width // (lax.axis_size("wide") * block_size)
    live_mask = (jnp.arange(slot_total, dtype=jnp.int32) < slot_count).astype(jnp.bfloat16)
    masked = stored * live_mask[:, None, None]
    dense_tile = jnp.zeros((row_blocks * col_blocks, block_size, block_size), jnp.bfloat16)
    dense_tile = dense_tile.at[places].add(masked)
    dense_tile = dense_tile.reshape(row_blocks, col_blocks, block_size, block_size)
    dense_tile = jnp.transpose(dense_tile, (0, 2, 1, 3)).reshape(row_blocks * block_size, col_blocks * block_size)
    gathered = lax.all_gather(t_amps, "wide", axis=0, tiled=True)
    partial_sum = jnp.dot(gathered, dense_tile, preferred_element_type=jnp.float32)
    return lax.psum_scatter(partial_sum, "narrow", scatter_dimension=0, tiled=True)


def ladder_kernel(depth, t, v_tile, meta_v, out, *scratch):
    held = scratch[: (2 * depth - 1) * PIECES]
    bufs = [held[b * PIECES:(b + 1) * PIECES] for b in range(2 * depth - 1)]
    (v_own, v_other, meta_in, meta, meta_other, runs, part, core_in, y_out, own_out, own_sem, lay_sem, bx_send, bx_recv, local_sem, az_send, az_recv, bz_send, bz_recv,
     ax_send, ax_recv, one_send, one_recv, core_send, core_recv, y_send, y_recv) = scratch[(2 * depth - 1) * PIECES:]
    wide, core = lax.axis_index("wide"), lax.axis_index("narrow")
    z, y, x = wide // 4, (wide // 2) % 2, wide % 2
    up, down = (wide + 4, core), (wide - 4, core)
    across = (wide + 1 - 2 * x, core)
    beside = (wide + 2 - 4 * y, core)
    twin = (wide, 1 - core)
    half = depth // 2
    rows, columns = t.shape
    v = v_tile.at[0, 0]
    slots, size = v.shape[0], v.shape[1]
    row_blocks = columns // size
    col_blocks = out.shape[-1] // size
    second = row_blocks * 4 // 32
    first = row_blocks - second
    chunk = rows // PIECES
    first_cols = pl.ds(0, first)
    second_cols = pl.ds(first, second)
    has_up, has_down = z < depth - 1, z > 0

    def copy(src, dst, send, recv, device):
        return pltpu.make_async_remote_copy(
            src_ref=src, dst_ref=dst, send_sem=send, recv_sem=recv, device_id=device, device_id_type=MESH
        )

    def place(b):
        if b == 0:
            return z, None
        if b < depth:
            return z - b, z >= b
        return z + (b - depth + 1), z + (b - depth + 1) < depth

    def guarded(cond, fn):
        if cond is None:
            fn()
        else:
            pl.when(cond)(fn)

    def both(a, b):
        return b if a is None else a if b is None else jnp.logical_and(a, b)

    def hops(b):
        moves = []
        if b < depth - 1:
            moves.append((b + 1, up, has_up, b))
        if b == 0 or depth <= b < 2 * depth - 2:
            landing = depth if b == 0 else b + 1
            moves.append((landing, down, has_down, depth - 1 + (landing - depth)))
        return moves

    def az(b, move, q):
        landing, device, unused, sem = move
        src = bufs[b][q].at[x, first_cols]
        return copy(src, bufs[landing][q].at[x, first_cols], az_send.at[sem, q], az_recv.at[landing, q], device)

    def bz(b, move, q):
        landing, device, unused, sem = move
        return copy(bufs[b][q].at[:, second_cols], bufs[landing][q].at[:, second_cols], bz_send.at[sem, q], bz_recv.at[landing, q], device)

    def ax(b, q):
        src = bufs[b][q].at[x, first_cols]
        return copy(src, src, ax_send.at[b, q], ax_recv.at[b, q], across)

    def az_wait(b, q):
        dst = bufs[b][q].at[x, first_cols]
        copy(dst, dst, az_send.at[0, q], az_recv.at[b, q], up).wait_recv()

    def bz_wait(b):
        for q in range(PIECES):
            dst = bufs[b][q].at[:, second_cols]
            copy(dst, dst, bz_send.at[0, q], bz_recv.at[b, q], up).wait_recv()

    def ax_wait(b, qs):
        for q in qs:
            dst = bufs[b][q].at[1 - x, first_cols]
            copy(dst, dst, ax_send.at[b, q], ax_recv.at[b, q], across).wait_recv()

    own_v = pltpu.make_async_copy(v, v_own, local_sem.at[1])
    own_m = pltpu.make_async_copy(meta_v, meta, local_sem.at[3])

    def lay(r, carry):
        at = pl.ds(pl.multiple_of(r * size, size), size)
        for q in range(PIECES):
            pltpu.make_async_copy(t.at[pl.ds(q * chunk, chunk), at], bufs[0][q].at[x, r], lay_sem.at[q]).start()
        return carry

    lax.fori_loop(0, row_blocks, lay, 0, unroll=8)
    own_v.start()
    own_m.start()
    barrier = pltpu.get_barrier_semaphore()
    for device in (across, beside, twin):
        pl.semaphore_signal(barrier, inc=1, device_id=device, device_id_type=MESH)
    pl.when(has_up)(lambda: pl.semaphore_signal(barrier, inc=1, device_id=up, device_id_type=MESH))
    pl.when(has_down)(lambda: pl.semaphore_signal(barrier, inc=1, device_id=down, device_id_type=MESH))
    pl.semaphore_wait(barrier, 3 + has_up.astype(jnp.int32) + has_down.astype(jnp.int32))

    bxs = [copy(bufs[0][q].at[x, second_cols], bufs[0][q].at[x, second_cols], bx_send.at[q], bx_recv.at[q], across)
           for q in range(PIECES)]
    vy = copy(v, v_other, one_send.at[1], one_recv.at[1], beside)
    my = copy(meta_v, meta_in, one_send.at[2], one_recv.at[2], beside)
    for q in range(PIECES):
        pltpu.make_async_copy(bufs[0][q].at[x], bufs[0][q].at[x], lay_sem.at[q]).wait()
    for bx in bxs:
        bx.start()
    for q in range(PIECES):
        for move in hops(0):
            guarded(move[2], lambda move=move, q=q: az(0, move, q).start())
        ax(0, q).start()
    my.start()
    vy.start()
    for bx in bxs:
        bx.wait_recv()

    def second_own(k):
        for move, turn in zip(hops(0), (z, depth - 1 - z)):
            guarded(both(move[2], turn == k), lambda move=move: [bz(0, move, q).start() for q in range(PIECES)] and None)

    def forward(b, q):
        def run():
            az_wait(b, q)
            for move in hops(b):
                guarded(move[2], lambda move=move: az(b, move, q).start())
            ax(b, q).start()

        guarded(place(b)[1], run)

    def forward_second(b):
        def run():
            bz_wait(b)
            for move in hops(b):
                guarded(move[2], lambda move=move: [bz(b, move, q).start() for q in range(PIECES)] and None)

        guarded(place(b)[1], run)

    def steps(b):
        if b in (depth - 1, 2 * depth - 2):
            return [(pl.ds(q * chunk, chunk), chunk, (q,)) for q in range(PIECES)]
        return [(pl.ds(0, rows), rows, tuple(range(PIECES)))]

    def products(b, strip, stored, info, span, count, qs):
        zp = place(b)[0]

        def slot(s, carry):
            at_row = info[1, s]
            left = jnp.concatenate([bufs[b][q][side, at_row] for side in (0, 1) for q in qs], axis=0)
            new = jnp.dot(left, stored[info[0, s]], preferred_element_type=jnp.float32)
            runs[s + 1, : 2 * count] = new + runs[s, : 2 * count] * info[2, s].astype(jnp.float32)
            return carry

        runs[0] = jnp.zeros((2 * rows, size), jnp.float32)
        lax.fori_loop(0, slots, slot, 0, unroll=8)
        for c in range(col_blocks):
            value = runs[info[3, c] + 1, : 2 * count] * info[4, c].astype(jnp.float32)
            part[zp, strip, :, span, c * size:(c + 1) * size] = value.reshape(2, count, size)

    def core_copy(b, strip, i):
        zp, span = place(b)[0], steps(b)[i][0]
        return copy(part.at[zp, strip, :, span], core_in.at[zp % half, strip, :, span],
                    core_send.at[b, strip, i], core_recv.at[b, strip, i], twin)

    def target(b, i):
        return out.at[place(b)[0] % half * 2 + y, :, steps(b)[i][0]]

    def y_copy(b, i):
        return copy(y_out.at[place(b)[0] % half, :, steps(b)[i][0]], target(b, i), y_send.at[b, i], y_recv.at[b, i], beside)

    def own_copy(b, i):
        zp, span = place(b)[0], steps(b)[i][0]
        return pltpu.make_async_copy(own_out.at[zp % half, :, span], target(b, i), own_sem.at[b, i])

    def mine(b):
        return place(b)[0] // half == core

    def compute(b, i):
        span, count, qs = steps(b)[i]

        def run():
            ax_wait(b, qs)
            for strip, stored, info in ((0, v_other, meta_other), (1, v_own, meta)):
                products(b, strip, stored, info, span, count, qs)
                pl.when(jnp.logical_not(mine(b)))(lambda strip=strip: core_copy(b, strip, i).start())

        guarded(place(b)[1], run)

    def finish(b, i):
        def run():
            zp, span = place(b)[0], steps(b)[i][0]
            slot = zp % half
            core_copy(b, 0, i).wait_recv()
            y_out[slot, :, span] = part[zp, 0, :, span] + core_in[slot, 0, :, span]
            y_copy(b, i).start()
            core_copy(b, 1, i).wait_recv()
            own_out[slot, :, span] = part[zp, 1, :, span] + core_in[slot, 1, :, span]
            own_copy(b, i).start()

        guarded(both(place(b)[1], mine(b)), run)

    def at(k):
        return [0] if k == 0 else [k, depth - 1 + k]

    second_own(0)
    for k in range(1, depth):
        for q in range(PIECES):
            for b in at(k):
                forward(b, q)
        second_own(k)
    own_v.wait()
    own_m.wait()
    my.wait_recv()
    into = pltpu.make_async_copy(meta_in, meta_other, local_sem.at[2])
    into.start()
    into.wait()
    vy.wait_recv()
    waiting = [(0, 0)]
    compute(0, 0)
    for k in range(1, depth):
        for b in at(k):
            forward_second(b)
        for i in range(len(steps(k))):
            for todo in waiting:
                finish(*todo)
            waiting = [(b, i) for b in at(k)]
            for todo in waiting:
                compute(*todo)
    for todo in waiting:
        finish(*todo)

    for bx in bxs:
        bx.wait_send()
    vy.wait_send()
    my.wait_send()
    for b in range(2 * depth - 1):
        valid = place(b)[1]
        for move in hops(b):
            guarded(both(valid, move[2]), lambda b=b, move=move: [(az(b, move, q).wait_send(), bz(b, move, q).wait_send()) for q in range(PIECES)] and None)
        guarded(valid, lambda b=b: [ax(b, q).wait_send() for q in range(PIECES)] and None)
        other = jnp.logical_not(mine(b))
        for i in range(len(steps(b))):
            guarded(both(valid, other), lambda b=b, i=i: [core_copy(b, j, i).wait_send() for j in (0, 1)] and None)
            guarded(both(valid, mine(b)), lambda b=b, i=i: [y_copy(b, i).wait(), own_copy(b, i).wait()] and None)


def slot_table(places, count, col_blocks):
    total = places.shape[0]
    ids = jnp.arange(total, dtype=jnp.int32)
    cols = jnp.where(ids < count, places % col_blocks, col_blocks)
    key = cols * total + ids
    rank = jnp.sum((key[None, :] < key[:, None]).astype(jnp.int32), axis=1)
    hit = (rank[:, None] == ids[None, :]).astype(jnp.int32)
    order = jnp.sum(hit * ids[:, None], axis=0)
    row = jnp.sum(hit * (places // col_blocks)[:, None], axis=0)
    col = jnp.sum(hit * cols[:, None], axis=0)
    before = jnp.sum((rank[:, None] + 1 == ids[None, :]).astype(jnp.int32) * (cols + 1)[:, None], axis=0) - 1
    same = (col == before).astype(jnp.int32)
    each = jnp.arange(col_blocks, dtype=jnp.int32)
    last = jnp.sum((cols[None, :] <= each[:, None]).astype(jnp.int32), axis=1) - 1
    some = jnp.sum((cols[None, :] == each[:, None]).astype(jnp.int32), axis=1)
    lanes = -(-max(total, col_blocks) // 128) * 128

    def wide(a):
        return jnp.pad(a, (0, lanes - a.shape[0]))

    zero = jnp.zeros((lanes,), jnp.int32)
    return jnp.stack([wide(order), wide(row), wide(same), wide(jnp.maximum(last, 0)), wide(jnp.minimum(some, 1)), zero, zero, zero])


def ring_shards(width, wide_size, t_amps, v_blocks, block_pos, block_count):
    rows, columns = t_amps.shape
    slots, size = v_blocks.shape[2], v_blocks.shape[3]
    depth = wide_size // 4
    half, buffers = depth // 2, 2 * depth - 1
    strip = width // wide_size
    meta = slot_table(block_pos[0, 0], block_count[0, 0], strip // size)
    bf16, f32, i32 = jnp.bfloat16, jnp.float32, jnp.int32
    dma = pltpu.SemaphoreType.DMA
    out = pl.pallas_call(
        functools.partial(ladder_kernel, depth),
        out_shape=jax.ShapeDtypeStruct((half * 2, 2, rows, strip), f32),
        in_specs=[
            pl.BlockSpec(memory_space=pl.ANY),
            pl.BlockSpec(memory_space=pl.ANY),
            pl.BlockSpec(memory_space=pltpu.VMEM),
        ],
        out_specs=pl.BlockSpec(memory_space=pl.ANY),
        scratch_shapes=[pltpu.VMEM((2, columns // size, rows // PIECES, size), bf16)] * (buffers * PIECES) + [
            pltpu.VMEM((slots, size, size), bf16),
            pltpu.VMEM((slots, size, size), bf16),
            pltpu.VMEM(meta.shape, i32),
            pltpu.SMEM(meta.shape, i32),
            pltpu.SMEM(meta.shape, i32),
            pltpu.VMEM((slots + 1, 2 * rows, size), f32),
            pltpu.VMEM((depth, 2, 2, rows, strip), f32),
            pltpu.VMEM((half, 2, 2, rows, strip), f32),
            pltpu.VMEM((half, 2, rows, strip), f32),
            pltpu.VMEM((half, 2, rows, strip), f32),
            dma((buffers, PIECES)),
            dma((PIECES,)), dma((PIECES,)), dma((PIECES,)),
            dma((4,)),
            dma((2 * depth, PIECES)), dma((buffers, PIECES)),
            dma((2 * depth, PIECES)), dma((buffers, PIECES)),
            dma((buffers, PIECES)), dma((buffers, PIECES)),
            dma((3,)), dma((3,)),
            dma((buffers, 2, PIECES)), dma((buffers, 2, PIECES)),
            dma((buffers, PIECES)), dma((buffers, PIECES)),
        ],
        compiler_params=pltpu.CompilerParams(
            collective_id=0, has_side_effects=True, vmem_limit_bytes=36 * 1024 * 1024
        ),
    )(t_amps, v_blocks, meta)
    return out.reshape(half * 4 * rows, strip)


def solution(mesh):
    in_specs = (
        P("wide", "narrow"),
        P("narrow", "wide", None, None, None),
        P("narrow", "wide", None),
        P("narrow", "wide"),
    )
    out_specs = P("narrow", "wide")
    wide_size, narrow_size = mesh.shape["wide"], mesh.shape["narrow"]

    def program(t_amps, v_blocks, block_pos, block_count):
        width = t_amps.shape[1]
        if narrow_size == 2 and wide_size % 8 == 0:
            body = functools.partial(ring_shards, width, wide_size)
        else:
            body = functools.partial(dense_shards, width)
        run = jax.shard_map(body, mesh=mesh, in_specs=in_specs, out_specs=out_specs, check_vma=False)
        return run(t_amps, v_blocks, block_pos, block_count)

    return program
```

time: 107 us -> 106 us (level); the launches traced: 107 us -> 104 us
  Pallas kernels: 99.8 us -> 98.4 us
    pallas_call x1, Pallas kernels: 99.8 us -> 98.4 us  [ring_shards(): pl.pallas_call(functools.partial(ladder_kernel, depth), out_shape=jax.Sha...]
    transpose x1 -> x0, local copies, waits for them, and re-layouts: 1.15 us -> none  [ring_shards(): jnp.transpose(t_amps.reshape(rows, columns // size, size), (1, 0, 2))]
    unnamed x3 -> x5, local copies, waits for them, and re-layouts: 3.14 us -> 4.13 us
where the time goes in v3:
time: 106 us; the launch traced here: 104 us
  Pallas kernels  98.4 us (93%)
  local copies, waits for them, and re-layouts  4.18 us (4%)
  other arithmetic  1.12 us (1%)
    pallas_call x1, Pallas kernels, ring_shards(): pl.pallas_call(functools.partial(ladder_kernel, depth), out_shape=jax.Sha...  98.4 us
    unnamed x5, local copies, waits for them, and re-layouts  4.13 us

profile of v3, /device:TPU:1, one launch (start us, length us, event | category | flops | bytes accessed | tf_op | source)
XLA Modules:
  0.0 104.4 jit_solution(2607885963217945033)
XLA Ops:
  0.7 0.7 broadcast_add_fusion
  1.3 0.2 convert_reduce_fusion
  1.5 0.1 select_reduce_fusion.1
  1.7 0.1 convert_reduce_fusion.1
  1.9 0.0 copy-start
  1.9 1.6 %copy-done = bf16[1,1,64,128,128]{4,3,2,1,0:T(8,128)(2,1)S(1)} copy-done((bf16[1,1,64,128,128]{4,3,2,1,0:T(8,128)(2,1)S(1)}, bf16[1,1,64,128,128]{4,3,2,1,0:T(8,128)(2,1)}, u32[]{:S(2)}) %copy-start) | copy-done | bytes 2097176
  3.5 0.0 copy-start.1
  3.5 1.2 %copy-done.1 = bf16[32,16384]{1,0:T(8,128)(2,1)S(1)} copy-done((bf16[32,16384]{1,0:T(8,128)(2,1)S(1)}, bf16[32,16384]{1,0:T(8,128)(2,1)}, u32[]{:S(2)}) %copy-start.1) | copy-done | bytes 1048600
  4.7 98.4 %shard_map.46 = f32[4,2,32,2048]{3,2,1,0:T(8,128)S(1)} custom-call(bf16[32,16384]{1,0:T(8,128)(2,1)S(1)} %copy-done.1, bf16[1,1,64,128,128]{4,3,2,1,0:T(8,128)(2,1)S(1)} %copy-done, s32[8,128]{1,0:T(8,128)S(1)} %stack.31.meta_v), custom_call_target="tpu_custom_call" | custom-call | tf_op jit(solution)/shard_map/pallas_call | solution.py:312
  103.1 1.3 %copy.7 = f32[256,2048]{1,0:T(8,128)} copy(f32[256,2048]{1,0:T(8,128)S(1)} %bitcast.29) | data formatting | bytes 4194304
  (12 shorter events, 0.1 us)
Async XLA Ops:
  1.9 1.6 %copy-start = (bf16[1,1,64,128,128]{4,3,2,1,0:T(8,128)(2,1)S(1)}, bf16[1,1,64,128,128]{4,3,2,1,0:T(8,128)(2,1)}, u32[]{:S(2)}) copy-start(bf16[1,1,64,128,128]{4,3,2,1,0:T(8,128)(2,1)} %v_tile.1) | copy-start | bytes 6291460
  3.5 1.2 %copy-start.1 = (bf16[32,16384]{1,0:T(8,128)(2,1)S(1)}, bf16[32,16384]{1,0:T(8,128)(2,1)}, u32[]{:S(2)}) copy-start(bf16[32,16384]{1,0:T(8,128)(2,1)} %t.1) | copy-start | bytes 3145732

commit v4 on v3

--- a/solution.py
+++ b/solution.py
@@ -42,14 +42,13 @@
     beside = (wide + 2 - 4 * y, core)
     twin = (wide, 1 - core)
     half = depth // 2
-    rows, columns = t.shape
+    pieces, row_blocks, chunk, unused = t.shape
+    rows = pieces * chunk
     v = v_tile.at[0, 0]
     slots, size = v.shape[0], v.shape[1]
-    row_blocks = columns // size
     col_blocks = out.shape[-1] // size
-    second = row_blocks * 4 // 32
+    second = row_blocks * 5 // 32
     first = row_blocks - second
-    chunk = rows // PIECES
     first_cols = pl.ds(0, first)
     second_cols = pl.ds(first, second)
     has_up, has_down = z < depth - 1, z > 0
@@ -86,7 +85,7 @@
 
     def az(b, move, q):
         landing, device, unused, sem = move
-        src = bufs[b][q].at[x, first_cols]
+        src = t.at[q, first_cols] if b == 0 else bufs[b][q].at[x, first_cols]
         return copy(src, bufs[landing][q].at[x, first_cols], az_send.at[sem, q], az_recv.at[landing, q], device)
 
     def bz(b, move, q):
@@ -94,8 +93,8 @@
         return copy(bufs[b][q].at[:, second_cols], bufs[landing][q].at[:, second_cols], bz_send.at[sem, q], bz_recv.at[landing, q], device)
 
     def ax(b, q):
-        src = bufs[b][q].at[x, first_cols]
-        return copy(src, src, ax_send.at[b, q], ax_recv.at[b, q], across)
+        src = t.at[q, first_cols] if b == 0 else bufs[b][q].at[x, first_cols]
+        return copy(src, bufs[b][q].at[x, first_cols], ax_send.at[b, q], ax_recv.at[b, q], across)
 
     def az_wait(b, q):
         dst = bufs[b][q].at[x, first_cols]
@@ -114,13 +113,9 @@
     own_v = pltpu.make_async_copy(v, v_own, local_sem.at[1])
     own_m = pltpu.make_async_copy(meta_v, meta, local_sem.at[3])
 
-    def lay(r, carry):
-        at = pl.ds(pl.multiple_of(r * size, size), size)
-        for q in range(PIECES):
-            pltpu.make_async_copy(t.at[pl.ds(q * chunk, chunk), at], bufs[0][q].at[x, r], lay_sem.at[q]).start()
-        return carry
-
-    lax.fori_loop(0, row_blocks, lay, 0, unroll=8)
+    lays = [pltpu.make_async_copy(t.at[q], bufs[0][q].at[x], lay_sem.at[q]) for q in range(PIECES)]
+    for lay in lays:
+        lay.start()
     own_v.start()
     own_m.start()
     barrier = pltpu.get_barrier_semaphore()
@@ -130,20 +125,19 @@
     pl.when(has_down)(lambda: pl.semaphore_signal(barrier, inc=1, device_id=down, device_id_type=MESH))
     pl.semaphore_wait(barrier, 3 + has_up.astype(jnp.int32) + has_down.astype(jnp.int32))
 
-    bxs = [copy(bufs[0][q].at[x, second_cols], bufs[0][q].at[x, second_cols], bx_send.at[q], bx_recv.at[q], across)
+    bxs = [copy(t.at[q, second_cols], bufs[0][q].at[x, second_cols], bx_send.at[q], bx_recv.at[q], across)
            for q in range(PIECES)]
     vy = copy(v, v_other, one_send.at[1], one_recv.at[1], beside)
     my = copy(meta_v, meta_in, one_send.at[2], one_recv.at[2], beside)
     for q in range(PIECES):
-        pltpu.make_async_copy(bufs[0][q].at[x], bufs[0][q].at[x], lay_sem.at[q]).wait()
-    for bx in bxs:
-        bx.start()
-    for q in range(PIECES):
+        bxs[q].start()
         for move in hops(0):
             guarded(move[2], lambda move=move, q=q: az(0, move, q).start())
         ax(0, q).start()
     my.start()
     vy.start()
+    for lay in lays:
+        lay.wait()
     for bx in bxs:
         bx.wait_recv()
 
@@ -307,6 +301,7 @@
     half, buffers = depth // 2, 2 * depth - 1
     strip = width // wide_size
     meta = slot_table(block_pos[0, 0], block_count[0, 0], strip // size)
+    by_piece = jnp.transpose(t_amps.reshape(PIECES, rows // PIECES, columns // size, size), (0, 2, 1, 3))
     bf16, f32, i32 = jnp.bfloat16, jnp.float32, jnp.int32
     dma = pltpu.SemaphoreType.DMA
     out = pl.pallas_call(
@@ -342,7 +337,7 @@
         compiler_params=pltpu.CompilerParams(
             collective_id=0, has_side_effects=True, vmem_limit_bytes=36 * 1024 * 1024
         ),
-    )(t_amps, v_blocks, meta)
+    )(by_piece, v_blocks, meta)
     return out.reshape(half * 4 * rows, strip)
 
 

time: 106 us -> 104 us (0.981); the launches traced: 104 us -> 104 us
    unnamed x5 -> x4, local copies, waits for them, and re-layouts: 4.13 us -> 2.94 us
where the time goes in v4:
time: 104 us
  Pallas kernels  98.4 us (95%)
  local copies, waits for them, and re-layouts  3.67 us (4%)
  other arithmetic  1.12 us (1%)
    pallas_call x1, Pallas kernels, ring_shards(): pl.pallas_call(functools.partial(ladder_kernel, depth), out_shape=jax.Sha...  98.4 us
    unnamed x4, local copies, waits for them, and re-layouts  2.94 us

profile of v4, /device:TPU:1, one launch (start us, length us, event | category | flops | bytes accessed | tf_op | source)
XLA Modules:
  0.0 104.0 jit_solution(16848245787834434508)
XLA Ops:
  0.7 0.7 broadcast_add_fusion
  1.3 0.2 convert_reduce_fusion
  1.5 0.1 select_reduce_fusion.1
  1.7 0.1 convert_reduce_fusion.1
  1.9 0.0 copy-start
  1.9 1.6 %copy.7 = bf16[4,8,128,128]{3,2,1,0:T(8,128)(2,1)S(1)} copy(bf16[4,8,128,128]{3,1,2,0:T(8,128)(2,1)} %bitcast.38) | data formatting | bytes 2097152
  3.5 0.7 copy.9
  4.2 0.0 copy-done
  4.2 98.4 %shard_map.46 = f32[4,2,32,2048]{3,2,1,0:T(8,128)S(1)} custom-call(bf16[2,128,16,128]{3,2,1,0:T(8,128)(2,1)S(1)} %bitcast.36, bf16[1,1,64,128,128]{4,3,2,1,0:T(8,128)(2,1)S(1)} %copy-done, s32[8,128]{1,0:T(8,128)S(1)} %stack.31.meta_v), custom_call_target="tpu_custom_call" | custom-call | tf_op jit(solution)/shard_map/pallas_call | solution.py:307
  102.7 1.3 %copy.12 = f32[256,2048]{1,0:T(8,128)} copy(f32[256,2048]{1,0:T(8,128)S(1)} %bitcast.35) | data formatting | bytes 4194304
  (12 shorter events, 0.1 us)
Async XLA Ops:
  1.9 2.3 %copy-start = (bf16[1,1,64,128,128]{4,3,2,1,0:T(8,128)(2,1)S(1)}, bf16[1,1,64,128,128]{4,3,2,1,0:T(8,128)(2,1)}, u32[]{:S(2)}) copy-start(bf16[1,1,64,128,128]{4,3,2,1,0:T(8,128)(2,1)} %v_tile.1) | copy-start | bytes 6291460
